TPU v7x, 512 devices: a whole 4x4x16 slice. The times are simulated.
512 devices in a mesh: dp: 32 (over z, core), fsdp: 16 (over x, y).
Axes of the slice: x: 4, y: 4, z: 16, core: 2. Of those that a mesh axis runs over, the one named last changes fastest.
Arguments:
- gradients: bfloat16 [1, 8192, 28672], P(None, 'fsdp', 'dp'), may hold values from -16 to 16
- errors: bfloat16 [1, 8192, 28672], P(None, 'fsdp', 'dp'), may hold values from -4 to 4
- start_factor: float32 [1, 32, 28672], P(None, None, 'dp'), may hold values from -6 to 6
Outputs:
- compressed: bfloat16 [1, 8192, 28672], P(None, 'fsdp', 'dp')
- new_errors: bfloat16 [1, 8192, 28672], P(None, 'fsdp', 'dp')
All inputs are finite; a program needn't handle non-finite values.
Results may differ from a plain program's by a relative error of at most 0.0085.
Values sent between devices are 32-bit elements; how exact they have to be, the bound alone decides.
No kernel may reach another device: no remote copies, remote signals or barrier semaphores. Data moves between devices by JAX's collectives and lax.ppermute only.
A program may use at most 64 MiB of HBM per device.

v0:
```python
import jax
import jax.numpy as jnp
from jax import lax
from jax.sharding import PartitionSpec as P


def orthonormal(lower, columns):

    def solve_single(factor, right_side):
        return jax.scipy.linalg.solve_triangular(factor, right_side, lower=True)

    return jax.vmap(solve_single)(lower, columns)


def shards(gradients, errors, start_factor):
    combined = (gradients.astype(jnp.float32) + errors.astype(jnp.float32)).astype(jnp.bfloat16)
    factor_low = start_factor.astype(jnp.bfloat16)
    products = jnp.einsum("mrc,mdc->mrd", factor_low, combined, preferred_element_type=jnp.float32)
    summed = lax.psum(products, "dp")
    whole = lax.all_gather(summed, "fsdp", axis=2, tiled=True)
    gram = jnp.einsum(
        "mrd,msd->mrs",
        whole,
        whole,
        precision=lax.Precision.HIGHEST,
        preferred_element_type=jnp.float32,
    )
    lower = jnp.linalg.cholesky(gram)
    basis = orthonormal(lower, summed)
    basis_low = basis.astype(jnp.bfloat16)
    projected = jnp.einsum("mrd,mdc->mrc", basis_low, combined, preferred_element_type=jnp.float32)
    factor_new = lax.psum(projected, "fsdp")
    rebuilt = jnp.einsum(
        "mrd,mrc->mdc",
        basis,
        factor_new,
        precision=lax.Precision.HIGHEST,
        preferred_element_type=jnp.float32,
    )
    compressed = rebuilt.astype(jnp.bfloat16)
    new_errors = (combined.astype(jnp.float32) - rebuilt).astype(jnp.bfloat16)
    return (compressed, new_errors)


def solution(mesh):
    placed = (P(None, "fsdp", "dp"), P(None, "fsdp", "dp"), P(None, None, "dp"))
    return jax.shard_map(
        shards,
        mesh=mesh,
        in_specs=placed,
        out_specs=(P(None, "fsdp", "dp"), P(None, "fsdp", "dp")),
        check_vma=False,
    )
```

profile of v0, /device:TPU:32, one launch (start us, length us, event | category | flops | bytes accessed | tf_op | source)
XLA Modules:
  0.0 389.8 jit_solution(7160317326725971944)
XLA Ops:
  7.2 0.0 all-reduce.3.cloned.1.call-start
  7.2 0.0 copy-start.1
  7.2 2.5 convolution_bitcast_fusion
  9.8 0.0 copy-start
  9.8 0.0 all-reduce.3.cloned.1.call-update
  9.8 0.0 all-gather.2.cloned.1.call-start
  9.8 190.7 %all-reduce.3.cloned.1.call-done = f32[1,32,512]{2,1,0:T(8,128)} async-done(((f32[1,32,512]{2,1,0:T(8,128)}), f32[1,32,512]{2,1,0:T(8,128)}) %all-reduce.3.cloned.1.call-update) | async-done | bytes 65552 | tf_op jit(solution)/shard_map/psum | solution.py:19
  200.5 0.0 copy-start.2
  200.5 0.0 all-gather.2.cloned.1.call-update
  200.5 0.0 all-reduce.5.cloned.1.call-start
  200.6 54.9 %all-gather.2.cloned.1.call-done = f32[1,32,8192]{2,1,0:T(8,128)} async-done(((f32[1,32,512]{2,1,0:T(8,128)}), f32[1,32,8192]{2,1,0:T(8,128)}) %all-gather.2.cloned.1.call-update) | async-done | bytes 1048592 | tf_op jit(solution)/shard_map/all_gather | solution.py:20
  255.5 2.5 fusion.1
  258.0 0.1 copy.6
  258.1 2.9 custom-call.8
  261.1 0.6 compare_reduce_fusion
  261.7 0.7 fusion.11
  262.4 2.4 custom-call.9
  264.8 0.0 copy-done.2
  264.8 0.3 fusion.6
  265.1 0.0 copy-done.1
  265.1 0.0 copy-done
  265.1 1.0 fusion.3
  266.1 0.0 all-reduce.5.cloned.1.call-update
  266.1 113.3 %all-reduce.5.cloned.1.call-done = f32[32,896]{1,0:T(8,128)} async-done(((f32[32,896]{1,0:T(8,128)}), f32[32,896]{1,0:T(8,128)}) %all-reduce.5.cloned.1.call-update) | async-done | bytes 114704 | tf_op jit(solution)/shard_map/psum | solution.py:32
  379.4 3.9 fusion
  (2 shorter events, 0.0 us)
Async XLA Ops:
  7.2 193.3 %all-reduce.3.cloned.1.call-start = ((), (), s32[]{:S(2)}) async-start(), calls=%async_computation | async-start | bytes 131072 | tf_op jit(solution)/shard_map/psum | solution.py:19
  7.2 257.9 %copy-start.1 = (bf16[1,512,896]{2,1,0:T(8,128)(2,1)S(1)}, bf16[1,512,896]{2,1,0:T(8,128)(2,1)}, u32[]{:S(2)}) copy-start(bf16[1,512,896]{2,1,0:T(8,128)(2,1)} %param.3) | copy-start | bytes 2752516
  9.8 255.3 %copy-start = (bf16[1,512,896]{2,1,0:T(8,128)(2,1)S(1)}, bf16[1,512,896]{2,1,0:T(8,128)(2,1)}, u32[]{:S(2)}) copy-start(bf16[1,512,896]{2,1,0:T(8,128)(2,1)} %param.4) | copy-start | bytes 2752516
  9.8 245.7 %all-gather.2.cloned.1.call-start = ((), (), s32[]{:S(2)}) async-start(), calls=%async_computation.1 | async-start | bytes 1114112 | tf_op jit(solution)/shard_map/all_gather | solution.py:20
  200.5 64.3 %copy-start.2 = (f32[1,32,512]{2,1,0:T(8,128)S(1)}, f32[1,32,512]{2,1,0:T(8,128)}, u32[]{:S(2)}) copy-start(f32[1,32,512]{2,1,0:T(8,128)} %all-reduce.3.cloned.1.call-done) | copy-start | bytes 196612
  200.5 178.9 %all-reduce.5.cloned.1.call-start = ((), (), s32[]{:S(2)}) async-start(), calls=%async_computation.2 | async-start | bytes 229376 | tf_op jit(solution)/shard_map/psum | solution.py:32
Sparse Core Ops, SparseCore 0:
  10.9 189.5 all-reduce.2
  203.6 51.8 all-gather.1
  266.2 113.1 all-reduce.4
where the time goes:
time: 390 us
  waiting for transfers between devices  359 us (92%)
  between operations  13.8 us (4%)
  matrix products  10.2 us (3%)
  other arithmetic  6.69 us (2%)
    psum x1, waiting for transfers between devices, shards(): summed = lax.psum(products, 'dp')  191 us
    psum x1, waiting for transfers between devices, shards(): factor_new = lax.psum(projected, 'fsdp')  113 us
    all_gather x1, waiting for transfers between devices, shards(): whole = lax.all_gather(summed, 'fsdp', axis=2, tiled=True)  54.9 us
  transfers between devices with their start and end apart: 3, of which 3 were waited for; matrix products, arithmetic and copies ran while one was open for 0% of the time, Pallas kernels for 0%

commit v1 on v0

--- a/solution.py
+++ b/solution.py
@@ -29,7 +29,8 @@
     basis = orthonormal(lower, summed)
     basis_low = basis.astype(jnp.bfloat16)
     projected = jnp.einsum("mrd,mdc->mrc", basis_low, combined, preferred_element_type=jnp.float32)
-    factor_new = lax.psum(projected, "fsdp")
+    parts = lax.all_gather(projected, "fsdp", axis=0, tiled=False)
+    factor_new = parts.sum(axis=0)
     rebuilt = jnp.einsum(
         "mrd,mrc->mdc",
         basis,

time: 390 us -> 338 us (0.87)
  the two profiles are of different devices: /device:TPU:32 before, /device:TPU:2 now
where the time goes in v1:
time: 338 us; the launch traced here: 337 us
  waiting for transfers between devices  305 us (90%)
  between operations  13.8 us (4%)
  matrix products  10.2 us (3%)
  other arithmetic  8.29 us (2%)
    psum x1, waiting for transfers between devices, shards(): summed = lax.psum(products, 'dp')  191 us
    all_gather x1, waiting for transfers between devices, shards(): parts = lax.all_gather(projected, 'fsdp', axis=0, tiled=False)  59.3 us
    all_gather x1, waiting for transfers between devices, shards(): whole = lax.all_gather(summed, 'fsdp', axis=2, tiled=True)  54.2 us
  transfers between devices with their start and end apart: 3, of which 3 were waited for; matrix products, arithmetic and copies ran while one was open for 0% of the time, Pallas kernels for 0%

profile of v1, /device:TPU:2, one launch (start us, length us, event | category | flops | bytes accessed | tf_op | source)
XLA Modules:
  0.0 337.4 jit_solution(15549703629740626446)
XLA Ops:
  7.2 0.0 copy-start
  7.2 0.0 copy-start.1
  7.2 0.0 all-reduce.2.cloned.1.call-start
  7.2 2.6 convolution_bitcast_fusion
  9.8 0.0 all-reduce.2.cloned.1.call-update
  9.8 0.0 all-gather.4.cloned.1.call-start
  9.9 191.4 %all-reduce.2.cloned.1.call-done = f32[1,32,512]{2,1,0:T(8,128)} async-done(((f32[1,32,512]{2,1,0:T(8,128)}), f32[1,32,512]{2,1,0:T(8,128)}) %all-reduce.2.cloned.1.call-update) | async-done | bytes 65552 | tf_op jit(solution)/shard_map/psum | solution.py:19
  201.3 0.0 all-gather.4.cloned.1.call-update
  201.3 0.0 all-gather.6.cloned.1.call-start
  201.4 54.2 %all-gather.4.cloned.1.call-done = f32[1,32,8192]{2,1,0:T(8,128)} async-done(((f32[1,32,512]{2,1,0:T(8,128)}), f32[1,32,8192]{2,1,0:T(8,128)}) %all-gather.4.cloned.1.call-update) | async-done | bytes 1048592 | tf_op jit(solution)/shard_map/all_gather | solution.py:20
  255.5 2.5 fusion.1
  258.1 0.1 copy.6
  258.1 2.9 custom-call.8
  261.1 0.6 compare_reduce_fusion
  261.7 0.7 fusion.11
  262.4 2.4 custom-call.9
  264.8 1.1 fusion.6
  266.0 0.0 copy-done
  266.0 0.0 copy-done.1
  266.0 1.0 fusion.3
  267.0 0.0 all-gather.6.cloned.1.call-update
  267.0 59.3 %all-gather.6.cloned.1.call-done = f32[512,896]{1,0:T(8,128)} async-done(((f32[32,896]{1,0:T(8,128)}), f32[512,896]{1,0:T(8,128)}) %all-gather.6.cloned.1.call-update) | async-done | bytes 1835024 | tf_op jit(solution)/shard_map/all_gather | solution.py:32
  326.3 1.6 reduce.10
  327.9 3.0 fusion
  (2 shorter events, 0.0 us)
Async XLA Ops:
  7.2 258.8 %copy-start = (bf16[1,512,896]{2,1,0:T(8,128)(2,1)S(1)}, bf16[1,512,896]{2,1,0:T(8,128)(2,1)}, u32[]{:S(2)}) copy-start(bf16[1,512,896]{2,1,0:T(8,128)(2,1)} %param.4) | copy-start | bytes 2752516
  7.2 258.8 %copy-start.1 = (bf16[1,512,896]{2,1,0:T(8,128)(2,1)S(1)}, bf16[1,512,896]{2,1,0:T(8,128)(2,1)}, u32[]{:S(2)}) copy-start(bf16[1,512,896]{2,1,0:T(8,128)(2,1)} %param.3) | copy-start | bytes 2752516
  7.2 194.1 %all-reduce.2.cloned.1.call-start = ((), (), s32[]{:S(2)}) async-start(), calls=%async_computation | async-start | bytes 131072 | tf_op jit(solution)/shard_map/psum | solution.py:19
  9.8 245.7 %all-gather.4.cloned.1.call-start = ((), (), s32[]{:S(2)}) async-start(), calls=%async_computation.1 | async-start | bytes 1114112 | tf_op jit(solution)/shard_map/all_gather | solution.py:20
  201.3 125.0 %all-gather.6.cloned.1.call-start = ((), (), s32[]{:S(2)}) async-start(), calls=%async_computation.2 | async-start | bytes 1949696 | tf_op jit(solution)/shard_map/all_gather | solution.py:32
Sparse Core Ops, SparseCore 0:
  10.9 190.3 all-reduce.1
  204.4 51.1 all-gather.3
  267.1 59.1 all-gather.5
